TPU v7x, 512 devices: a whole 4x4x16 slice. The times are simulated.
512 devices in a mesh: dp: 16 (over z), expert: 32 (over y, x, core).
Axes of the slice: x: 4, y: 4, z: 16, core: 2. Of those that a mesh axis runs over, the one named last changes fastest.
Arguments:
- tokens: bfloat16 [4096, 4096], P('expert', 'dp'), may hold values from -6 to 6
- routing: int32 [4096, 8], P('expert'), may hold values from 0 to 31, all different within a row; in each aligned block of 128 rows (0 to 127, 128 to 255, ...) at most 40 rows name the same one
- gate_probs: float32 [4096, 8], P('expert'), may hold values from 0.05 to 0.3
- paired: int32 [32], P('expert'), may hold values from 0 to 1, as said below
- w_gate: bfloat16 [32, 4096, 768], P('expert', 'dp'), may hold values from -0.09375 to 0.09375
- w_up: bfloat16 [32, 4096, 768], P('expert', 'dp'), may hold values from -0.09375 to 0.09375
- w_down: bfloat16 [32, 768, 4096], P('expert', None, 'dp'), may hold values from -0.21875 to 0.21875
- cotangent: bfloat16 [4096, 4096], P('expert', 'dp'), may hold values from -6 to 6
Outputs:
- output: bfloat16 [4096, 4096], P('expert', 'dp')
- grad_tokens: bfloat16 [4096, 4096], P('expert', 'dp')
- grad_gate: float32 [32, 4096, 768], P('expert', 'dp')
- grad_up: float32 [32, 4096, 768], P('expert', 'dp')
- grad_down: float32 [32, 768, 4096], P('expert', None, 'dp')
Inputs may be any that keep to these rules, and one draw needn't show every extreme that they name: `routing`: each token names 8 different copies; among the tokens of one source (aligned blocks of 128 tokens) no copy is named more than 40 times, a bound that some block reaches. paired[c] equals paired[(c + 16) mod 32]; paired[0] and paired[31] are 1.
All inputs are finite; a program needn't handle non-finite values.
Results may differ from a plain program's by a relative error of at most 0.029.
Values may be sent and summed in bfloat16 or wider, within the bound.
A program may use at most 64 MiB of HBM per device.

v0:
```python
import jax
import jax.numpy as jnp
from jax import lax
from jax.sharding import PartitionSpec as P


def swapped(value, axis, stride):
    mask = 2**stride
    pairs = [(source, source ^ mask) for source in range(lax.axis_size(axis))]
    return lax.ppermute(value, axis, pairs)


def product(left, right):
    return jnp.dot(left, right, preferred_element_type=jnp.float32)


def inner_rows(left, right):
    return lax.dot_general(
        left, right, (((0,), (0,)), ((), ())), preferred_element_type=jnp.float32
    )


def outer_cols(left, right):
    return lax.dot_general(
        left, right, (((1,), (1,)), ((), ())), preferred_element_type=jnp.float32
    )


def rounded(value):
    return lax.optimization_barrier(value.astype(jnp.bfloat16)).astype(jnp.float32)


def per_device(tokens, routing, gate_probs, paired, w_gate, w_up, w_down, cotangent):
    n_expert = lax.axis_size("expert")
    n_data = lax.axis_size("dp")
    token_count, top_count = routing.shape
    slab = tokens.shape[1]
    hidden = w_gate.shape[2]
    capacity = max(2, 5 * token_count * top_count // (4 * n_expert))
    all_rows = n_expert * capacity
    own_rows = all_rows // n_data
    gate_slab = w_gate[0]
    up_slab = w_up[0]
    down_slab = w_down[0]
    flat_route = routing.reshape(token_count * top_count)
    onehot = (flat_route[:, None] == jnp.arange(n_expert, dtype=jnp.int32)[None, :]).astype(
        jnp.int32
    )
    earlier = jnp.cumsum(onehot, axis=0) - onehot
    target = flat_route * capacity + jnp.sum(earlier * onehot, axis=1)
    select = jnp.arange(all_rows, dtype=jnp.int32)[:, None] == target[None, :]
    select_grid = select.reshape(all_rows, token_count, top_count)
    token_select = jnp.any(select_grid, axis=2).astype(jnp.bfloat16)
    weight_select = jnp.sum(select_grid.astype(jnp.float32) * gate_probs[None, :, :], axis=2)
    weight_high = weight_select.astype(jnp.bfloat16)
    weight_low = (weight_select - weight_high.astype(jnp.float32)).astype(jnp.bfloat16)
    send_tokens = product(token_select, tokens).astype(jnp.bfloat16)
    scaled = (gate_probs[:, :, None] * cotangent.astype(jnp.float32)[:, None, :]).astype(
        jnp.bfloat16
    )
    send_grads = product(
        select.astype(jnp.bfloat16), scaled.reshape(token_count * top_count, slab)
    ).astype(jnp.bfloat16)
    arrived = (
        lax.all_to_all(
            send_tokens.reshape(n_expert, capacity, slab),
            "expert",
            split_axis=0,
            concat_axis=0,
            tiled=True,
        ),
        lax.all_to_all(
            send_grads.reshape(n_expert, capacity, slab),
            "expert",
            split_axis=0,
            concat_axis=0,
            tiled=True,
        ),
    )
    token_slab = arrived[0].reshape(all_rows, slab)
    grad_slab = arrived[1].reshape(all_rows, slab)
    block_rows = token_slab
    summed = lax.psum_scatter(
        rounded(
            jnp.concatenate([product(block_rows, gate_slab), product(block_rows, up_slab)], axis=1)
        ).astype(jnp.bfloat16),
        "dp",
        scatter_dimension=0,
        tiled=True,
    ).astype(jnp.float32)
    gate_own = summed[:, :hidden]
    up_own = summed[:, hidden:]
    hid_own = (jax.nn.silu(gate_own) * up_own).astype(jnp.bfloat16)
    piece = lax.all_gather(hid_own, "dp", axis=0, tiled=True)
    answer_acc = product(piece, down_slab)
    grad_down = inner_rows(piece, grad_slab)
    answer_slab = answer_acc.astype(jnp.bfloat16)
    answer_back = lax.all_to_all(
        answer_slab.reshape(n_expert, capacity, slab),
        "expert",
        split_axis=0,
        concat_axis=0,
        tiled=True,
    )
    hidden_parts = (
        outer_cols(grad_slab, down_slab).astype(jnp.bfloat16).reshape(n_data, own_rows, hidden)
    )
    arrived_parts = lax.all_to_all(hidden_parts, "dp", split_axis=0, concat_axis=0, tiled=True)
    grad_hidden = jnp.sum(arrived_parts.astype(jnp.float32), axis=0)
    sigma = jax.nn.sigmoid(gate_own)
    activated = gate_own * sigma
    grad_gate_rows = (grad_hidden * up_own * sigma * (1.0 + gate_own * (1.0 - sigma))).astype(
        jnp.bfloat16
    )
    grad_up_rows = (grad_hidden * activated).astype(jnp.bfloat16)
    piece_gate = lax.all_gather(grad_gate_rows, "dp", axis=0, tiled=True)
    piece_up = lax.all_gather(grad_up_rows, "dp", axis=0, tiled=True)
    block_rows = token_slab
    gate_acc = inner_rows(block_rows, piece_gate)
    up_acc = inner_rows(block_rows, piece_up)
    back_rows = outer_cols(piece_gate, gate_slab) + outer_cols(piece_up, up_slab)
    grad_gate = gate_acc
    grad_up = up_acc
    back_slab = back_rows.astype(jnp.bfloat16)
    back_rows_home = lax.all_to_all(
        back_slab.reshape(n_expert, capacity, slab),
        "expert",
        split_axis=0,
        concat_axis=0,
        tiled=True,
    )
    answer_home = answer_back.reshape(all_rows, slab)
    output = (inner_rows(weight_high, answer_home) + inner_rows(weight_low, answer_home)).astype(
        jnp.bfloat16
    )
    grad_tokens = inner_rows(token_select, back_rows_home.reshape(all_rows, slab)).astype(
        jnp.bfloat16
    )
    other = (
        swapped(grad_gate.astype(jnp.bfloat16), "expert", n_expert.bit_length() - 2).astype(
            grad_gate.dtype
        ),
        swapped(grad_up.astype(jnp.bfloat16), "expert", n_expert.bit_length() - 2).astype(
            grad_up.dtype
        ),
        swapped(grad_down.astype(jnp.bfloat16), "expert", n_expert.bit_length() - 2).astype(
            grad_down.dtype
        ),
    )
    keep = paired.astype(jnp.float32)[0]
    grad_gate = (grad_gate + keep * other[0])[None]
    grad_up = (grad_up + keep * other[1])[None]
    grad_down = (grad_down + keep * other[2])[None]
    return (output, grad_tokens, grad_gate, grad_up, grad_down)


def solution(mesh):
    return jax.shard_map(
        per_device,
        mesh=mesh,
        in_specs=(
            P("expert", "dp"),
            P("expert", None),
            P("expert", None),
            P("expert"),
            P("expert", "dp", None),
            P("expert", "dp", None),
            P("expert", None, "dp"),
            P("expert", "dp"),
        ),
        out_specs=(
            P("expert", "dp"),
            P("expert", "dp"),
            P("expert", "dp", None),
            P("expert", "dp", None),
            P("expert", None, "dp"),
        ),
        check_vma=False,
    )
```

profile of v0, /device:TPU:1, one launch (start us, length us, event | category | flops | bytes accessed | tf_op | source)
XLA Modules:
  0.0 480.7 jit_solution(16176602574999856850)
XLA Ops:
  7.2 0.0 copy-start
  7.2 0.8 copy.41
  8.0 0.1 eq.50
  8.1 0.1 eq.46
  8.2 0.0 copy-start.12
  8.2 9.0 %reduce-window.6 = s32[32,8,128]{2,1,0:T(8,128)S(1)} reduce-window(s32[32,8,128]{2,1,0:T(8,128)S(1)} %fusion.24, s32[]{:T(128)} %constant.7.clone.1), window={size=1x1x128 pad=0_0x0_0x127_0}, to_apply=%region_0.0 | reduce-window | flops 4161536 | bytes 262148 | tf_op jit(solution)/shard_map/reduce-window
  17.3 0.1 slice.16
  17.4 0.1 copy.43
  17.5 0.1 copy.44
  17.6 0.1 broadcast_add_fusion
  17.8 0.1 reduce_sum.30
  17.9 0.7 multiply_add_fusion.1
  18.6 4.6 fusion
  23.3 2.1 convolution_convert_fusion.4
  25.3 10.4 %all-to-all-start = ((bf16[32,40,256]{2,1,0:T(8,128)(2,1)}), bf16[32,40,256]{2,1,0:T(8,128)(2,1)S(1)}, u32[]{:S(2)}, u32[]{:S(2)}) async-start(bf16[32,40,256]{2,1,0:T(8,128)(2,1)} %bitcast.2), calls=%async_computation | async-start | bytes 1310720 | tf_op jit(solution)/shard_map/all_to_all | solution.py:65
  35.8 0.1 copy.47
  35.9 0.1 mul.92
  36.0 0.0 copy-start.6
  36.0 1.9 fusion.4
  38.0 10.8 %all-to-all-done = bf16[32,40,256]{2,1,0:T(8,128)(2,1)S(1)} async-done(((bf16[32,40,256]{2,1,0:T(8,128)(2,1)}), bf16[32,40,256]{2,1,0:T(8,128)(2,1)S(1)}, u32[]{:S(2)}, u32[]{:S(2)}) %all-to-all-start) | async-done | bytes 655392 | tf_op jit(solution)/shard_map/all_to_all | solution.py:65
  48.8 4.2 all-to-all-start.2
  53.0 0.0 reduce-scatter.4.cloned.1.call-start
  53.1 0.7 convolution_convert_fusion.1
  53.8 0.7 convolution_convert_fusion.2
  54.5 2.1 pad_maximum_fusion
  56.7 6.3 %copy.48 = bf16[1280,1536]{1,0:T(8,128)(2,1)} copy(bf16[1280,1536]{0,1:T(8,128)(2,1)} %pad_maximum_fusion) | data formatting | bytes 7864320
  63.0 0.0 reduce-scatter.4.cloned.1.call-update
  63.0 0.0 all-gather.4.cloned.1.call-start
  63.0 3.0 all-to-all-done.2
  66.1 0.7 convolution_convert_fusion
  66.8 117.4 %all_to_all.25 = bf16[16,80,768]{2,1,0:T(8,128)(2,1)S(1)} all-to-all(bf16[16,80,768]{2,1,0:T(8,128)(2,1)S(1)} %bitcast.77), channel_id=1, replica_groups=mesh['dp'=16,'expert'=32] {'dp'}, dimensions={0} | all-to-all | bytes 3932160 | tf_op jit(solution)/shard_map/all_to_all | solution.py:108
  184.2 0.3 convert_reduce_fusion
  184.5 27.7 %reduce-scatter.4.cloned.1.call-done = bf16[80,1536]{1,0:T(8,128)(2,1)} async-done(((bf16[1280,1536]{1,0:T(8,128)(2,1)}), bf16[80,1536]{1,0:T(8,128)(2,1)}) %reduce-scatter.4.cloned.1.call-update) | async-done | bytes 245776 | tf_op jit(solution)/shard_map/reduce_scatter | solution.py:83
  212.2 1.0 convert_element_type.90
  213.2 0.9 multiply_convert_fusion
  214.1 0.0 all-gather.4.cloned.1.call-update
  214.1 0.0 all-gather.6.cloned.1.call-start
  214.1 0.7 all-gather.6.cloned.1.call-update
  214.8 0.2 all-gather.8.cloned.1.call-start
  215.1 0.3 all-gather.8.cloned.1.call-update
  216.1 6.8 %select_reduce_fusion = f32[1280,128]{1,0:T(8,128)S(1)} fusion(f32[128,8]{0,1:T(8,128)S(1)} %copy-done.12, s32[128,8]{0,1:T(8,128)S(1)} %multiply_add_fusion.1), kind=kLoop, calls=%fused_computation.1 | loop fusion | flops 3768320 | bytes 663552 | tf_op jit(solution)/shard_map/reduce_sum | solution.py:54
  222.8 56.5 %all-gather.4.cloned.1.call-done = bf16[1280,768]{1,0:T(8,128)(2,1)} async-done(((bf16[80,768]{1,0:T(8,128)(2,1)}), bf16[1280,768]{1,0:T(8,128)(2,1)}) %all-gather.4.cloned.1.call-update) | async-done | bytes 1966096 | tf_op jit(solution)/shard_map/all_gather | solution.py:94
  279.3 3.1 convolution_convert_fusion.3
  282.4 17.4 %all-to-all-start.1 = ((bf16[32,40,256]{2,1,0:T(8,128)(2,1)}), bf16[32,40,256]{2,1,0:T(8,128)(2,1)S(1)}, u32[]{:S(2)}, u32[]{:S(2)}) async-start(bf16[32,40,256]{2,1,0:T(8,128)(2,1)} %bitcast.7), calls=%async_computation.1 | async-start | bytes 1310720 | tf_op jit(solution)/shard_map/all_to_all | solution.py:98
  299.7 52.7 %all-gather.6.cloned.1.call-done = bf16[1280,768]{1,0:T(8,128)(2,1)} async-done(((bf16[80,768]{1,0:T(8,128)(2,1)}), bf16[1280,768]{1,0:T(8,128)(2,1)}) %all-gather.6.cloned.1.call-update) | async-done | bytes 1966096 | tf_op jit(solution)/shard_map/all_gather | solution.py:116
  352.4 3.0 fusion.25
  355.4 4.6 collective-permute-start
  360.1 64.6 %all-gather.8.cloned.1.call-done = bf16[1280,768]{1,0:T(8,128)(2,1)} async-done(((bf16[80,768]{1,0:T(8,128)(2,1)}), bf16[1280,768]{1,0:T(8,128)(2,1)}) %all-gather.8.cloned.1.call-update) | async-done | bytes 1966096 | tf_op jit(solution)/shard_map/all_gather | solution.py:117
  424.7 2.4 fusion.26
  427.1 4.8 collective-permute-start.1
  431.9 1.7 fusion.27
  433.6 2.3 collective-permute-start.2
  435.9 0.7 fusion.14
  436.6 1.6 fusion.3
  438.2 0.0 collective-permute-done
  438.2 2.0 add_bitcast_fusion.2
  440.2 0.0 collective-permute-done.1
  440.2 1.0 add_bitcast_fusion.1
  441.1 18.0 %all-to-all-start.4 = ((bf16[32,40,256]{2,1,0:T(8,128)(2,1)}), bf16[32,40,256]{2,1,0:T(8,128)(2,1)}, u32[]{:S(2)}, u32[]{:S(2)}) async-start(bf16[32,40,256]{2,1,0:T(8,128)(2,1)} %bitcast.13), calls=%async_computation.4 | async-start | bytes 1310720 | tf_op jit(solution)/shard_map/all_to_all | solution.py:125
  459.1 2.0 add_bitcast_fusion
  461.1 0.3 fusion.19
  461.4 0.9 fusion.5
  462.3 9.8 %all-to-all-done.4 = bf16[32,40,256]{2,1,0:T(8,128)(2,1)} async-done(((bf16[32,40,256]{2,1,0:T(8,128)(2,1)}), bf16[32,40,256]{2,1,0:T(8,128)(2,1)}, u32[]{:S(2)}, u32[]{:S(2)}) %all-to-all-start.4) | async-done | bytes 655392 | tf_op jit(solution)/shard_map/all_to_all | solution.py:125
  472.1 2.1 convolution_convert_fusion.5
  (34 shorter events, 0.2 us)
Async XLA Ops:
  7.2 58.9 %copy-start = (bf16[1,768,256]{2,1,0:T(8,128)(2,1)S(1)}, bf16[1,768,256]{2,1,0:T(8,128)(2,1)}, u32[]{:S(2)}) copy-start(bf16[1,768,256]{2,1,0:T(8,128)(2,1)} %param.14) | copy-start | bytes 1179652
  8.0 27.8 %copy-start.11 = (bf16[128,256]{1,0:T(8,128)(2,1)S(1)}, bf16[128,256]{1,0:T(8,128)(2,1)}, u32[]{:S(2)}) copy-start(bf16[128,256]{1,0:T(8,128)(2,1)} %param.15) | copy-start | bytes 196612
  8.2 27.6 %copy-start.12 = (f32[128,8]{0,1:T(8,128)S(1)}, f32[128,8]{0,1:T(8,128)}, u32[]{:S(2)}) copy-start(f32[128,8]{0,1:T(8,128)} %param.10) | copy-start | bytes 12292
  23.3 2.1 copy-start.9
  25.3 23.5 %all-to-all-start = ((bf16[32,40,256]{2,1,0:T(8,128)(2,1)}), bf16[32,40,256]{2,1,0:T(8,128)(2,1)S(1)}, u32[]{:S(2)}, u32[]{:S(2)}) async-start(bf16[32,40,256]{2,1,0:T(8,128)(2,1)} %bitcast.2), calls=%async_computation | async-start | bytes 1310720 | tf_op jit(solution)/shard_map/all_to_all | solution.py:65
  36.0 17.1 %copy-start.6 = (bf16[1,256,768]{2,1,0:T(8,128)(2,1)S(1)}, bf16[1,256,768]{2,1,0:T(8,128)(2,1)}, u32[]{:S(2)}) copy-start(bf16[1,256,768]{2,1,0:T(8,128)(2,1)} %param.13) | copy-start | bytes 1179652
  48.8 5.0 %copy-start.5 = (bf16[1,256,768]{2,1,0:T(8,128)(2,1)S(1)}, bf16[1,256,768]{2,1,0:T(8,128)(2,1)}, u32[]{:S(2)}) copy-start(bf16[1,256,768]{2,1,0:T(8,128)(2,1)} %param.12) | copy-start | bytes 1179652
  48.8 17.3 %all-to-all-start.2 = ((bf16[32,40,256]{2,1,0:T(8,128)(2,1)}), bf16[32,40,256]{2,1,0:T(8,128)(2,1)S(1)}, u32[]{:S(2)}, u32[]{:S(2)}) async-start(bf16[32,40,256]{2,1,0:T(8,128)(2,1)} %bitcast.10), calls=%async_computation.2 | async-start | bytes 1310720 | tf_op jit(solution)/shard_map/all_to_all | solution.py:72
  53.0 159.2 %reduce-scatter.4.cloned.1.call-start = ((), (), s32[]{:S(2)}) async-start(), calls=%async_computation.9 | async-start | bytes 4177920 | tf_op jit(solution)/shard_map/reduce_scatter | solution.py:83
  63.0 216.3 %all-gather.4.cloned.1.call-start = ((), (), s32[]{:S(2)}) async-start(), calls=%async_computation.6 | async-start | bytes 2088960 | tf_op jit(solution)/shard_map/all_gather | solution.py:94
  66.1 118.1 %copy-start.3 = (bf16[32,40,256]{2,1,0:T(8,128)(2,1)}, bf16[32,40,256]{2,1,0:T(8,128)(2,1)S(1)}, u32[]{:S(2)}) copy-start(bf16[32,40,256]{2,1,0:T(8,128)(2,1)S(1)} %all-to-all-done.2) | copy-start | bytes 1966084
  214.1 138.3 %all-gather.6.cloned.1.call-start = ((), (), s32[]{:S(2)}) async-start(), calls=%async_computation.7 | async-start | bytes 2088960 | tf_op jit(solution)/shard_map/all_gather | solution.py:116
  214.8 209.8 %all-gather.8.cloned.1.call-start = ((), (), s32[]{:S(2)}) async-start(), calls=%async_computation.8 | async-start | bytes 2088960 | tf_op jit(solution)/shard_map/all_gather | solution.py:117
  282.4 158.8 %all-to-all-start.1 = ((bf16[32,40,256]{2,1,0:T(8,128)(2,1)}), bf16[32,40,256]{2,1,0:T(8,128)(2,1)S(1)}, u32[]{:S(2)}, u32[]{:S(2)}) async-start(bf16[32,40,256]{2,1,0:T(8,128)(2,1)} %bitcast.7), calls=%async_computation.1 | async-start | bytes 1310720 | tf_op jit(solution)/shard_map/all_to_all | solution.py:98
  355.4 82.8 %collective-permute-start = (bf16[256,768]{1,0:T(8,128)(2,1)}, bf16[256,768]{1,0:T(8,128)(2,1)}, u32[]{:S(2)}, u32[]{:S(2)}) collective-permute-start(bf16[256,768]{1,0:T(8,128)(2,1)} %get-tuple-element.8), channel_id=1, source_target_pairs={{0,16},{1,17},{2,18},{3,19},{4,20},{5,21},{6,22},{7,23},{8,24},{9,... | collective-permute-start | bytes 1179656 | tf_op jit(solution)/shard_map/ppermute | solution.py:10
  424.7 7.2 %copy-start.4 = (bf16[32,40,256]{2,1,0:T(8,128)(2,1)S(1)}, bf16[32,40,256]{2,1,0:T(8,128)(2,1)}, u32[]{:S(2)}) copy-start(bf16[32,40,256]{2,1,0:T(8,128)(2,1)} %copy-done.3) | copy-start | bytes 1966084
  424.7 7.2 %copy-start.13 = (bf16[1280,768]{1,0:T(8,128)(2,1)S(1)}, bf16[1280,768]{1,0:T(8,128)(2,1)}, u32[]{:S(2)}) copy-start(bf16[1280,768]{1,0:T(8,128)(2,1)} %all-gather.4.cloned.1.call-done) | copy-start | bytes 5898244
  427.1 8.8 %copy-start.1 = (bf16[1280,768]{1,0:T(8,128)(2,1)S(1)}, bf16[1280,768]{1,0:T(8,128)(2,1)}, u32[]{:S(2)}) copy-start(bf16[1280,768]{1,0:T(8,128)(2,1)} %all-gather.6.cloned.1.call-done) | copy-start | bytes 5898244
  427.1 13.1 %collective-permute-start.1 = (bf16[256,768]{1,0:T(8,128)(2,1)S(1)}, bf16[256,768]{1,0:T(8,128)(2,1)S(1)}, u32[]{:S(2)}, u32[]{:S(2)}) collective-permute-start(bf16[256,768]{1,0:T(8,128)(2,1)S(1)} %get-tuple-element.10), channel_id=1, source_target_pairs={{0,16},{1,17},{2,18},{3,19},{4,20},{5,21},{6,22},{7,23},{8,24},{9,... | collective-permute-start | bytes 1179656 | tf_op jit(solution)/shard_map/ppermute | solution.py:10
  433.6 3.0 copy-start.2
  433.6 3.0 copy-start.7
  433.6 25.5 %collective-permute-start.2 = (bf16[768,256]{1,0:T(8,128)(2,1)}, bf16[768,256]{1,0:T(8,128)(2,1)}, u32[]{:S(2)}, u32[]{:S(2)}) collective-permute-start(bf16[768,256]{1,0:T(8,128)(2,1)} %get-tuple-element.12), channel_id=1, source_target_pairs={{0,16},{1,17},{2,18},{3,19},{4,20},{5,21},{6,22},{7,23},{8,24},{9,... | collective-permute-start | bytes 1179656 | tf_op jit(solution)/shard_map/ppermute | solution.py:10
  440.2 19.0 %copy-start.8 = (f32[768,256]{1,0:T(8,128)S(1)}, f32[768,256]{1,0:T(8,128)}, u32[]{:S(2)}) copy-start(f32[768,256]{1,0:T(8,128)} %get-tuple-element.13) | copy-start | bytes 2359300
  441.1 30.9 %all-to-all-start.4 = ((bf16[32,40,256]{2,1,0:T(8,128)(2,1)}), bf16[32,40,256]{2,1,0:T(8,128)(2,1)}, u32[]{:S(2)}, u32[]{:S(2)}) async-start(bf16[32,40,256]{2,1,0:T(8,128)(2,1)} %bitcast.13), calls=%async_computation.4 | async-start | bytes 1310720 | tf_op jit(solution)/shard_map/all_to_all | solution.py:125
  461.1 11.0 %copy-start.10 = (pred[1280,128]{1,0:T(8,128)(4,1)S(1)}, pred[1280,128]{1,0:T(8,128)(4,1)}, u32[]{:S(2)}) copy-start(pred[1280,128]{1,0:T(8,128)(4,1)} %copy-done.9) | copy-start | bytes 491524
Sparse Core Ops, SparseCore 0:
  63.1 149.0 reduce-scatter.3
  214.5 64.7 all-gather.3
  282.1 70.2 all-gather.5
  355.2 69.4 all-gather.7
where the time goes:
time: 482 us; the launch traced here: 481 us
  waiting for transfers between devices  226 us (47%)
  blocking collectives  117 us (24%)
  starting transfers between devices  62 us (13%)
  other arithmetic  30.5 us (6%)
  matrix products  22 us (5%)
  between operations  14.7 us (3%)
  local copies, waits for them, and re-layouts  7.99 us (2%)
    all_to_all x1, blocking collectives, per_device(): lax.all_to_all(hidden_parts, 'dp', split_axis=0, concat_axis=0, tiled=True)  117 us
    all_gather x1, waiting for transfers between devices, per_device(): piece_up = lax.all_gather(grad_up_rows, 'dp', axis=0, tiled=True)  64.6 us
    all_gather x1, waiting for transfers between devices, per_device(): piece = lax.all_gather(hid_own, 'dp', axis=0, tiled=True)  56.5 us
    all_gather x1, waiting for transfers between devices, per_device(): piece_gate = lax.all_gather(grad_gate_rows, 'dp', axis=0, tiled=True)  52.7 us
    reduce_scatter x1, waiting for transfers between devices, per_device(): lax.psum_scatter(rounded(jnp.concatenate([product(block_rows, gate_slab),...  27.7 us
    all_to_all x1, starting transfers between devices, per_device(): lax.all_to_all(back_slab.reshape(n_expert, capacity, slab), 'expert', spl...  18 us
    all_to_all x1, starting transfers between devices, per_device(): lax.all_to_all(answer_slab.reshape(n_expert, capacity, slab), 'expert', s...  17.4 us
    ppermute x3, starting transfers between devices, swapped(): return lax.ppermute(value, axis, pairs)  11.7 us
  transfers between devices with their start and end apart: 11, of which 7 were waited for; matrix products, arithmetic and copies ran while one was open for 8% of the time, Pallas kernels for 0%

commit v1 on v0

--- a/solution.py
+++ b/solution.py
@@ -2,6 +2,12 @@
 import jax.numpy as jnp
 from jax import lax
 from jax.sharding import PartitionSpec as P
+
+
+def laid_out(pieces, dim):
+    shape = list(pieces.shape[1:])
+    shape[dim] *= pieces.shape[0]
+    return jnp.moveaxis(pieces, 0, dim).reshape(shape)
 
 
 def swapped(value, axis, stride):
@@ -114,7 +120,19 @@
     )
     grad_up_rows = (grad_hidden * activated).astype(jnp.bfloat16)
     piece_gate = lax.all_gather(grad_gate_rows, "dp", axis=0, tiled=True)
-    piece_up = lax.all_gather(grad_up_rows, "dp", axis=0, tiled=True)
+    size = lax.axis_size("dp")
+    pairs_2 = [(i, (i + 1) % size) for i in range(size)]
+    back = [(b, a) for a, b in pairs_2]
+    lower, upper = ([], [])
+    for step in range(size - 1):
+        if step % 2 == 0:
+            lower.append(lax.ppermute(lower[-1] if lower else grad_up_rows, "dp", pairs_2))
+        else:
+            upper.append(lax.ppermute(upper[-1] if upper else grad_up_rows, "dp", back))
+    pieces = jnp.stack([*lower[::-1], grad_up_rows, *upper])
+    shift = lax.axis_index("dp") - len(lower)
+    pieces = pieces[(jnp.arange(size) - shift) % size]
+    piece_up = laid_out(pieces, 0)
     block_rows = token_slab
     gate_acc = inner_rows(block_rows, piece_gate)
     up_acc = inner_rows(block_rows, piece_up)

time: 482 us -> 401 us (0.83)
  waiting for transfers between devices: 226 us -> 82.1 us
  starting transfers between devices: 62 us -> 111 us
  local copies, waits for them, and re-layouts: 7.99 us -> 20.7 us
    all_gather x1 -> x0, waiting for transfers between devices: 64.6 us -> none  [per_device(): piece_up = lax.all_gather(grad_up_rows, 'dp', axis=0, tiled=True)]
    all_gather x1, waiting for transfers between devices: 52.7 us -> 0.01 us  [per_device(): piece_gate = lax.all_gather(grad_gate_rows, 'dp', axis=0, tiled=True)]
    ppermute x0 -> x15, starting transfers between devices: none -> 49.4 us  [the longest x7 32.9 us: per_device(): upper.append(lax.ppermute(upper[-1] if upper else grad_up_rows, 'dp', back))]
    all_gather x1, waiting for transfers between devices: 56.5 us -> 21.1 us  [per_device(): piece = lax.all_gather(hid_own, 'dp', axis=0, tiled=True)]
    ppermute x0 -> x15, waiting for transfers between devices: none -> 12.6 us  [the longest x8 11.2 us: per_device(): lax.ppermute(lower[-1] if lower else grad_up_rows, 'dp', pairs_2)]
    unnamed x31 -> x42, local copies, waits for them, and re-layouts: 7.29 us -> 17.2 us
    all_to_all x1, waiting for transfers between devices: 9.76 us -> 0.01 us  [per_device(): lax.all_to_all(back_slab.reshape(n_expert, capacity, slab), 'expert', spl...]
    all_to_all x1, waiting for transfers between devices: 0.01 us -> 6.78 us  [per_device(): lax.all_to_all(answer_slab.reshape(n_expert, capacity, slab), 'expert', s...]
  transfers between devices with their start and end apart: 11 -> 25, of which waited for: 7 -> 16; matrix products, arithmetic and copies ran while one was open for 8% -> 13% of each run, Pallas kernels for 0% -> 0%
where the time goes in v1:
time: 401 us; the launch traced here: 399 us
  blocking collectives  117 us (29%)
  starting transfers between devices  111 us (28%)
  waiting for transfers between devices  82.1 us (20%)
  other arithmetic  31.4 us (8%)
  matrix products  21.8 us (5%)
  local copies, waits for them, and re-layouts  20.7 us (5%)
  between operations  14.9 us (4%)
    all_to_all x1, blocking collectives, per_device(): lax.all_to_all(hidden_parts, 'dp', split_axis=0, concat_axis=0, tiled=True)  117 us
    ppermute x7, starting transfers between devices, per_device(): upper.append(lax.ppermute(upper[-1] if upper else grad_up_rows, 'dp', back))  32.9 us
    reduce_scatter x1, waiting for transfers between devices, per_device(): lax.psum_scatter(rounded(jnp.concatenate([product(block_rows, gate_slab),...  27.7 us
    all_gather x1, waiting for transfers between devices, per_device(): piece = lax.all_gather(hid_own, 'dp', axis=0, tiled=True)  21.1 us
    all_to_all x1, starting transfers between devices, per_device(): lax.all_to_all(back_slab.reshape(n_expert, capacity, slab), 'expert', spl...  19 us
    unnamed x42, local copies, waits for them, and re-layouts  17.2 us
    ppermute x8, starting transfers between devices, per_device(): lax.ppermute(lower[-1] if lower else grad_up_rows, 'dp', pairs_2)  16.5 us
    all_to_all x1, starting transfers between devices, per_device(): lax.all_to_all(answer_slab.reshape(n_expert, capacity, slab), 'expert', s...  15.1 us
  transfers between devices with their start and end apart: 25, of which 16 were waited for; matrix products, arithmetic and copies ran while one was open for 13% of the time, Pallas kernels for 0%

profile of v1, /device:TPU:1, one launch (start us, length us, event | category | flops | bytes accessed | tf_op | source)
XLA Modules:
  0.0 399.5 jit_solution(3356113379425192773)
XLA Ops:
  7.2 0.8 copy.42
  8.2 9.0 %reduce-window.6 = s32[32,8,128]{2,1,0:T(8,128)S(1)} reduce-window(s32[32,8,128]{2,1,0:T(8,128)S(1)} %fusion.24, s32[]{:T(128)} %constant.33.clone.1), window={size=1x1x128 pad=0_0x0_0x127_0}, to_apply=%region_0.0 | reduce-window | flops 4161536 | bytes 262148 | tf_op jit(solution)/shard_map/reduce-window
  17.9 0.7 multiply_add_fusion.1
  18.6 4.6 %fusion = pred[1280,128]{1,0:T(8,128)(4,1)S(1)} fusion(s32[128,8]{0,1:T(8,128)S(1)} %multiply_add_fusion.1), kind=kLoop, calls=%fused_computation.4 | loop fusion | flops 2457600 | bytes 167936 | tf_op jit(solution)/shard_map/reduce_or | solution.py:59
  23.3 2.1 convolution_convert_fusion.4
  25.3 10.4 %all-to-all-start = ((bf16[32,40,256]{2,1,0:T(8,128)(2,1)}), bf16[32,40,256]{2,1,0:T(8,128)(2,1)S(1)}, u32[]{:S(2)}, u32[]{:S(2)}) async-start(bf16[32,40,256]{2,1,0:T(8,128)(2,1)} %bitcast.2), calls=%async_computation | async-start | bytes 1310720 | tf_op jit(solution)/shard_map/all_to_all | solution.py:71
  36.0 1.9 fusion.4
  38.0 10.8 %all-to-all-done = bf16[32,40,256]{2,1,0:T(8,128)(2,1)S(1)} async-done(((bf16[32,40,256]{2,1,0:T(8,128)(2,1)}), bf16[32,40,256]{2,1,0:T(8,128)(2,1)S(1)}, u32[]{:S(2)}, u32[]{:S(2)}) %all-to-all-start) | async-done | bytes 655392 | tf_op jit(solution)/shard_map/all_to_all | solution.py:71
  48.8 4.1 %all-to-all-start.2 = ((bf16[32,40,256]{2,1,0:T(8,128)(2,1)}), bf16[32,40,256]{2,1,0:T(8,128)(2,1)S(1)}, u32[]{:S(2)}, u32[]{:S(2)}) async-start(bf16[32,40,256]{2,1,0:T(8,128)(2,1)} %bitcast.10), calls=%async_computation.2 | async-start | bytes 1310720 | tf_op jit(solution)/shard_map/all_to_all | solution.py:78
  53.0 0.7 convolution_convert_fusion.1
  53.7 0.7 convolution_convert_fusion.2
  54.4 2.2 pad_maximum_fusion
  56.6 6.3 %copy.49 = bf16[1280,1536]{1,0:T(8,128)(2,1)} copy(bf16[1280,1536]{0,1:T(8,128)(2,1)} %pad_maximum_fusion) | data formatting | bytes 7864320
  62.9 3.0 all-to-all-done.2
  65.9 0.7 convolution_convert_fusion
  66.6 117.4 %all_to_all.25 = bf16[16,80,768]{2,1,0:T(8,128)(2,1)S(1)} all-to-all(bf16[16,80,768]{2,1,0:T(8,128)(2,1)S(1)} %bitcast.114), channel_id=1, replica_groups=mesh['dp'=16,'expert'=32] {'dp'}, dimensions={0} | all-to-all | bytes 3932160 | tf_op jit(solution)/shard_map/all_to_all | solution.py:114
  184.3 27.7 %reduce-scatter.4.cloned.1.call-done = bf16[80,1536]{1,0:T(8,128)(2,1)} async-done(((bf16[1280,1536]{1,0:T(8,128)(2,1)}), bf16[80,1536]{1,0:T(8,128)(2,1)}) %reduce-scatter.4.cloned.1.call-update) | async-done | bytes 245776 | tf_op jit(solution)/shard_map/reduce_scatter | solution.py:89
  212.0 1.0 convert_element_type.90
  212.9 0.8 multiply_convert_fusion
  213.8 3.1 collective-permute-start
  217.0 3.7 collective-permute-done
  220.7 1.9 collective-permute-start.1
  222.6 4.6 %collective-permute-start.8 = (bf16[80,768]{1,0:T(8,128)(2,1)S(1)}, bf16[80,768]{1,0:T(8,128)(2,1)S(1)}, u32[]{:S(2)}, u32[]{:S(2)}) collective-permute-start(bf16[80,768]{1,0:T(8,128)(2,1)S(1)} %get-tuple-element.5), channel_id=1, source_target_pairs={{32,0},{64,32},{96,64},{128,96},{160,128},{192,160},{224,192},{256... | collective-permute-start | bytes 368648 | tf_op jit(solution)/shard_map/ppermute | solution.py:131
  227.2 0.7 collective-permute-done.1
  227.9 1.9 collective-permute-start.2
  229.8 4.6 %collective-permute-start.9 = (bf16[80,768]{1,0:T(8,128)(2,1)S(1)}, bf16[80,768]{1,0:T(8,128)(2,1)S(1)}, u32[]{:S(2)}, u32[]{:S(2)}) collective-permute-start(bf16[80,768]{1,0:T(8,128)(2,1)S(1)} %collective-permute-done.8), channel_id=1, source_target_pairs={{32,0},{64,32},{96,64},{128,96},{160,128},{192,160},{224,192},{256... | collective-permute-start | bytes 368648 | tf_op jit(solution)/shard_map/ppermute | solution.py:131
  234.4 1.7 collective-permute-done.2
  236.1 1.9 collective-permute-start.3
  238.0 5.3 %collective-permute-start.10 = (bf16[80,768]{1,0:T(8,128)(2,1)S(1)}, bf16[80,768]{1,0:T(8,128)(2,1)S(1)}, u32[]{:S(2)}, u32[]{:S(2)}) collective-permute-start(bf16[80,768]{1,0:T(8,128)(2,1)S(1)} %collective-permute-done.9), channel_id=1, source_target_pairs={{32,0},{64,32},{96,64},{128,96},{160,128},{192,160},{224,192},{256... | collective-permute-start | bytes 368648 | tf_op jit(solution)/shard_map/ppermute | solution.py:131
  243.3 1.9 collective-permute-done.3
  245.2 1.9 collective-permute-start.4
  247.1 5.2 %collective-permute-start.11 = (bf16[80,768]{1,0:T(8,128)(2,1)S(1)}, bf16[80,768]{1,0:T(8,128)(2,1)S(1)}, u32[]{:S(2)}, u32[]{:S(2)}) collective-permute-start(bf16[80,768]{1,0:T(8,128)(2,1)S(1)} %collective-permute-done.10), channel_id=1, source_target_pairs={{32,0},{64,32},{96,64},{128,96},{160,128},{192,160},{224,192},{256... | collective-permute-start | bytes 368648 | tf_op jit(solution)/shard_map/ppermute | solution.py:131
  252.7 2.0 collective-permute-start.5
  255.1 4.6 %collective-permute-start.12 = (bf16[80,768]{1,0:T(8,128)(2,1)S(1)}, bf16[80,768]{1,0:T(8,128)(2,1)S(1)}, u32[]{:S(2)}, u32[]{:S(2)}) collective-permute-start(bf16[80,768]{1,0:T(8,128)(2,1)S(1)} %collective-permute-done.11), channel_id=1, source_target_pairs={{32,0},{64,32},{96,64},{128,96},{160,128},{192,160},{224,192},{256... | collective-permute-start | bytes 368648 | tf_op jit(solution)/shard_map/ppermute | solution.py:131
  260.2 1.9 collective-permute-start.6
  262.2 0.7 collective-permute-done.12
  262.8 4.4 %collective-permute-start.13 = (bf16[80,768]{1,0:T(8,128)(2,1)S(1)}, bf16[80,768]{1,0:T(8,128)(2,1)S(1)}, u32[]{:S(2)}, u32[]{:S(2)}) collective-permute-start(bf16[80,768]{1,0:T(8,128)(2,1)S(1)} %collective-permute-done.12), channel_id=1, source_target_pairs={{32,0},{64,32},{96,64},{128,96},{160,128},{192,160},{224,192},{256... | collective-permute-start | bytes 368648 | tf_op jit(solution)/shard_map/ppermute | solution.py:131
  267.2 0.9 collective-permute-done.6
  268.1 1.9 collective-permute-start.7
  270.4 4.4 %collective-permute-start.14 = (bf16[80,768]{1,0:T(8,128)(2,1)S(1)}, bf16[80,768]{1,0:T(8,128)(2,1)S(1)}, u32[]{:S(2)}, u32[]{:S(2)}) collective-permute-start(bf16[80,768]{1,0:T(8,128)(2,1)S(1)} %collective-permute-done.13), channel_id=1, source_target_pairs={{32,0},{64,32},{96,64},{128,96},{160,128},{192,160},{224,192},{256... | collective-permute-start | bytes 368648 | tf_op jit(solution)/shard_map/ppermute | solution.py:131
  274.8 1.3 collective-permute-done.7
  276.1 0.7 bitcast_dynamic-update-slice_fusion.15
  278.7 0.7 bitcast_dynamic-update-slice_fusion.11
  282.0 0.7 bitcast_dynamic-update-slice_fusion.6
  286.6 2.2 gather_fusion
  288.9 0.7 fusion.28
  289.6 3.9 collective-permute-start.16
  294.1 7.6 %select_reduce_fusion = f32[1280,128]{1,0:T(8,128)} fusion(f32[128,8]{0,1:T(8,128)S(1)} %copy-done.10, s32[128,8]{0,1:T(8,128)S(1)} %multiply_add_fusion.1), kind=kLoop, calls=%fused_computation.2 | loop fusion | flops 3768320 | bytes 663552 | tf_op jit(solution)/shard_map/reduce_sum | solution.py:60
  301.7 1.0 add_bitcast_fusion.1
  302.7 2.3 fusion.14
  304.9 1.6 fusion.3
  306.5 19.0 %all-to-all-start.4 = ((bf16[32,40,256]{2,1,0:T(8,128)(2,1)}), bf16[32,40,256]{2,1,0:T(8,128)(2,1)}, u32[]{:S(2)}, u32[]{:S(2)}) async-start(bf16[32,40,256]{2,1,0:T(8,128)(2,1)} %bitcast.119), calls=%async_computation.4 | async-start | bytes 1310720 | tf_op jit(solution)/shard_map/all_to_all | solution.py:143
  325.5 3.1 fusion.27
  328.5 4.9 %collective-permute-start.15 = (bf16[256,768]{1,0:T(8,128)(2,1)}, bf16[256,768]{1,0:T(8,128)(2,1)}, u32[]{:S(2)}, u32[]{:S(2)}) collective-permute-start(bf16[256,768]{1,0:T(8,128)(2,1)} %get-tuple-element.8), channel_id=1, source_target_pairs={{0,16},{1,17},{2,18},{3,19},{4,20},{5,21},{6,22},{7,23},{8,24},{9,... | collective-permute-start | bytes 1179656 | tf_op jit(solution)/shard_map/ppermute | solution.py:16
  333.5 21.1 %all-gather.3.cloned.1.call-done = bf16[1280,768]{1,0:T(8,128)(2,1)} async-done(((bf16[80,768]{1,0:T(8,128)(2,1)}), bf16[1280,768]{1,0:T(8,128)(2,1)}) %all-gather.3.cloned.1.call-update) | async-done | bytes 1966096 | tf_op jit(solution)/shard_map/all_gather | solution.py:100
  354.6 3.2 fusion.29
  357.8 4.3 %collective-permute-start.17 = (bf16[768,256]{1,0:T(8,128)(2,1)}, bf16[768,256]{1,0:T(8,128)(2,1)}, u32[]{:S(2)}, u32[]{:S(2)}) collective-permute-start(bf16[768,256]{1,0:T(8,128)(2,1)} %get-tuple-element.12), channel_id=1, source_target_pairs={{0,16},{1,17},{2,18},{3,19},{4,20},{5,21},{6,22},{7,23},{8,24},{9,... | collective-permute-start | bytes 1179656 | tf_op jit(solution)/shard_map/ppermute | solution.py:16
  362.1 1.5 convolution_convert_fusion.3
  363.7 15.1 %all-to-all-start.1 = ((bf16[32,40,256]{2,1,0:T(8,128)(2,1)}), bf16[32,40,256]{2,1,0:T(8,128)(2,1)S(1)}, u32[]{:S(2)}, u32[]{:S(2)}) async-start(bf16[32,40,256]{2,1,0:T(8,128)(2,1)} %bitcast.7), calls=%async_computation.1 | async-start | bytes 1310720 | tf_op jit(solution)/shard_map/all_to_all | solution.py:104
  378.8 2.0 add_bitcast_fusion.2
  380.9 2.0 add_bitcast_fusion
  382.8 2.1 convolution_convert_fusion.5
  384.9 6.8 %all-to-all-done.1 = bf16[32,40,256]{2,1,0:T(8,128)(2,1)S(1)} async-done(((bf16[32,40,256]{2,1,0:T(8,128)(2,1)}), bf16[32,40,256]{2,1,0:T(8,128)(2,1)S(1)}, u32[]{:S(2)}, u32[]{:S(2)}) %all-to-all-start.1) | async-done | bytes 655392 | tf_op jit(solution)/shard_map/all_to_all | solution.py:104
  392.0 0.9 fusion.5
  (76 shorter events, 12.1 us)
Async XLA Ops:
  7.2 46.5 %copy-start = (bf16[1,256,768]{2,1,0:T(8,128)(2,1)S(1)}, bf16[1,256,768]{2,1,0:T(8,128)(2,1)}, u32[]{:S(2)}) copy-start(bf16[1,256,768]{2,1,0:T(8,128)(2,1)} %param.12) | copy-start | bytes 1179652
  8.0 27.8 %copy-start.9 = (bf16[128,256]{1,0:T(8,128)(2,1)S(1)}, bf16[128,256]{1,0:T(8,128)(2,1)}, u32[]{:S(2)}) copy-start(bf16[128,256]{1,0:T(8,128)(2,1)} %param.15) | copy-start | bytes 196612
  8.2 27.6 %copy-start.10 = (f32[128,8]{0,1:T(8,128)S(1)}, f32[128,8]{0,1:T(8,128)}, u32[]{:S(2)}) copy-start(f32[128,8]{0,1:T(8,128)} %param.10) | copy-start | bytes 12292
  23.3 2.1 copy-start.5
  25.3 23.5 %all-to-all-start = ((bf16[32,40,256]{2,1,0:T(8,128)(2,1)}), bf16[32,40,256]{2,1,0:T(8,128)(2,1)S(1)}, u32[]{:S(2)}, u32[]{:S(2)}) async-start(bf16[32,40,256]{2,1,0:T(8,128)(2,1)} %bitcast.2), calls=%async_computation | async-start | bytes 1310720 | tf_op jit(solution)/shard_map/all_to_all | solution.py:71
  36.0 16.9 %copy-start.4 = (bf16[1,256,768]{2,1,0:T(8,128)(2,1)S(1)}, bf16[1,256,768]{2,1,0:T(8,128)(2,1)}, u32[]{:S(2)}) copy-start(bf16[1,256,768]{2,1,0:T(8,128)(2,1)} %param.13) | copy-start | bytes 1179652
  48.8 17.1 %all-to-all-start.2 = ((bf16[32,40,256]{2,1,0:T(8,128)(2,1)}), bf16[32,40,256]{2,1,0:T(8,128)(2,1)S(1)}, u32[]{:S(2)}, u32[]{:S(2)}) async-start(bf16[32,40,256]{2,1,0:T(8,128)(2,1)} %bitcast.10), calls=%async_computation.2 | async-start | bytes 1310720 | tf_op jit(solution)/shard_map/all_to_all | solution.py:78
  52.9 159.1 %reduce-scatter.4.cloned.1.call-start = ((), (), s32[]{:S(2)}) async-start(), calls=%async_computation.8 | async-start | bytes 4177920 | tf_op jit(solution)/shard_map/reduce_scatter | solution.py:89
  62.8 3.1 copy-start.7
  62.9 239.8 %all-gather.5.cloned.1.call-start = ((), (), s32[]{:S(2)}) async-start(), calls=%async_computation.7 | async-start | bytes 2088960 | tf_op jit(solution)/shard_map/all_gather | solution.py:122
  65.9 118.1 %copy-start.2 = (bf16[32,40,256]{2,1,0:T(8,128)(2,1)}, bf16[32,40,256]{2,1,0:T(8,128)(2,1)S(1)}, u32[]{:S(2)}) copy-start(bf16[32,40,256]{2,1,0:T(8,128)(2,1)S(1)} %all-to-all-done.2) | copy-start | bytes 1966084
  213.8 140.8 %all-gather.3.cloned.1.call-start = ((), (), s32[]{:S(2)}) async-start(), calls=%async_computation.6 | async-start | bytes 2088960 | tf_op jit(solution)/shard_map/all_gather | solution.py:100
  213.8 6.8 %collective-permute-start = (bf16[80,768]{1,0:T(8,128)(2,1)S(1)}, bf16[80,768]{1,0:T(8,128)(2,1)S(1)}, u32[]{:S(2)}, u32[]{:S(2)}) collective-permute-start(bf16[80,768]{1,0:T(8,128)(2,1)S(1)} %get-tuple-element.5), channel_id=1, source_target_pairs={{0,32},{32,64},{64,96},{96,128},{128,160},{160,192},{192,224},{224... | collective-permute-start | bytes 368648 | tf_op jit(solution)/shard_map/ppermute | solution.py:129
  220.7 7.2 %collective-permute-start.1 = (bf16[80,768]{1,0:T(8,128)(2,1)S(1)}, bf16[80,768]{1,0:T(8,128)(2,1)S(1)}, u32[]{:S(2)}, u32[]{:S(2)}) collective-permute-start(bf16[80,768]{1,0:T(8,128)(2,1)S(1)} %collective-permute-done), channel_id=1, source_target_pairs={{0,32},{32,64},{64,96},{96,128},{128,160},{160,192},{192,224},{224... | collective-permute-start | bytes 368648 | tf_op jit(solution)/shard_map/ppermute | solution.py:129
  222.6 7.2 %collective-permute-start.8 = (bf16[80,768]{1,0:T(8,128)(2,1)S(1)}, bf16[80,768]{1,0:T(8,128)(2,1)S(1)}, u32[]{:S(2)}, u32[]{:S(2)}) collective-permute-start(bf16[80,768]{1,0:T(8,128)(2,1)S(1)} %get-tuple-element.5), channel_id=1, source_target_pairs={{32,0},{64,32},{96,64},{128,96},{160,128},{192,160},{224,192},{256... | collective-permute-start | bytes 368648 | tf_op jit(solution)/shard_map/ppermute | solution.py:131
  227.9 8.2 %collective-permute-start.2 = (bf16[80,768]{1,0:T(8,128)(2,1)S(1)}, bf16[80,768]{1,0:T(8,128)(2,1)S(1)}, u32[]{:S(2)}, u32[]{:S(2)}) collective-permute-start(bf16[80,768]{1,0:T(8,128)(2,1)S(1)} %collective-permute-done.1), channel_id=1, source_target_pairs={{0,32},{32,64},{64,96},{96,128},{128,160},{160,192},{192,224},{224... | collective-permute-start | bytes 368648 | tf_op jit(solution)/shard_map/ppermute | solution.py:129
  229.8 8.2 %collective-permute-start.9 = (bf16[80,768]{1,0:T(8,128)(2,1)S(1)}, bf16[80,768]{1,0:T(8,128)(2,1)S(1)}, u32[]{:S(2)}, u32[]{:S(2)}) collective-permute-start(bf16[80,768]{1,0:T(8,128)(2,1)S(1)} %collective-permute-done.8), channel_id=1, source_target_pairs={{32,0},{64,32},{96,64},{128,96},{160,128},{192,160},{224,192},{256... | collective-permute-start | bytes 368648 | tf_op jit(solution)/shard_map/ppermute | solution.py:131
  236.1 9.1 %collective-permute-start.3 = (bf16[80,768]{1,0:T(8,128)(2,1)S(1)}, bf16[80,768]{1,0:T(8,128)(2,1)S(1)}, u32[]{:S(2)}, u32[]{:S(2)}) collective-permute-start(bf16[80,768]{1,0:T(8,128)(2,1)S(1)} %collective-permute-done.2), channel_id=1, source_target_pairs={{0,32},{32,64},{64,96},{96,128},{128,160},{160,192},{192,224},{224... | collective-permute-start | bytes 368648 | tf_op jit(solution)/shard_map/ppermute | solution.py:129
  238.0 9.1 %collective-permute-start.10 = (bf16[80,768]{1,0:T(8,128)(2,1)S(1)}, bf16[80,768]{1,0:T(8,128)(2,1)S(1)}, u32[]{:S(2)}, u32[]{:S(2)}) collective-permute-start(bf16[80,768]{1,0:T(8,128)(2,1)S(1)} %collective-permute-done.9), channel_id=1, source_target_pairs={{32,0},{64,32},{96,64},{128,96},{160,128},{192,160},{224,192},{256... | collective-permute-start | bytes 368648 | tf_op jit(solution)/shard_map/ppermute | solution.py:131
  245.2 7.5 %collective-permute-start.4 = (bf16[80,768]{1,0:T(8,128)(2,1)S(1)}, bf16[80,768]{1,0:T(8,128)(2,1)S(1)}, u32[]{:S(2)}, u32[]{:S(2)}) collective-permute-start(bf16[80,768]{1,0:T(8,128)(2,1)S(1)} %collective-permute-done.3), channel_id=1, source_target_pairs={{0,32},{32,64},{64,96},{96,128},{128,160},{160,192},{192,224},{224... | collective-permute-start | bytes 368648 | tf_op jit(solution)/shard_map/ppermute | solution.py:129
  247.1 7.9 %collective-permute-start.11 = (bf16[80,768]{1,0:T(8,128)(2,1)S(1)}, bf16[80,768]{1,0:T(8,128)(2,1)S(1)}, u32[]{:S(2)}, u32[]{:S(2)}) collective-permute-start(bf16[80,768]{1,0:T(8,128)(2,1)S(1)} %collective-permute-done.10), channel_id=1, source_target_pairs={{32,0},{64,32},{96,64},{128,96},{160,128},{192,160},{224,192},{256... | collective-permute-start | bytes 368648 | tf_op jit(solution)/shard_map/ppermute | solution.py:131
  252.7 7.5 %collective-permute-start.5 = (bf16[80,768]{1,0:T(8,128)(2,1)S(1)}, bf16[80,768]{1,0:T(8,128)(2,1)S(1)}, u32[]{:S(2)}, u32[]{:S(2)}) collective-permute-start(bf16[80,768]{1,0:T(8,128)(2,1)S(1)} %collective-permute-done.4), channel_id=1, source_target_pairs={{0,32},{32,64},{64,96},{96,128},{128,160},{160,192},{192,224},{224... | collective-permute-start | bytes 368648 | tf_op jit(solution)/shard_map/ppermute | solution.py:129
  255.1 7.8 %collective-permute-start.12 = (bf16[80,768]{1,0:T(8,128)(2,1)S(1)}, bf16[80,768]{1,0:T(8,128)(2,1)S(1)}, u32[]{:S(2)}, u32[]{:S(2)}) collective-permute-start(bf16[80,768]{1,0:T(8,128)(2,1)S(1)} %collective-permute-done.11), channel_id=1, source_target_pairs={{32,0},{64,32},{96,64},{128,96},{160,128},{192,160},{224,192},{256... | collective-permute-start | bytes 368648 | tf_op jit(solution)/shard_map/ppermute | solution.py:131
  260.2 7.8 %collective-permute-start.6 = (bf16[80,768]{1,0:T(8,128)(2,1)S(1)}, bf16[80,768]{1,0:T(8,128)(2,1)S(1)}, u32[]{:S(2)}, u32[]{:S(2)}) collective-permute-start(bf16[80,768]{1,0:T(8,128)(2,1)S(1)} %collective-permute-done.5), channel_id=1, source_target_pairs={{0,32},{32,64},{64,96},{96,128},{128,160},{160,192},{192,224},{224... | collective-permute-start | bytes 368648 | tf_op jit(solution)/shard_map/ppermute | solution.py:129
  262.8 7.6 %collective-permute-start.13 = (bf16[80,768]{1,0:T(8,128)(2,1)S(1)}, bf16[80,768]{1,0:T(8,128)(2,1)S(1)}, u32[]{:S(2)}, u32[]{:S(2)}) collective-permute-start(bf16[80,768]{1,0:T(8,128)(2,1)S(1)} %collective-permute-done.12), channel_id=1, source_target_pairs={{32,0},{64,32},{96,64},{128,96},{160,128},{192,160},{224,192},{256... | collective-permute-start | bytes 368648 | tf_op jit(solution)/shard_map/ppermute | solution.py:131
  268.1 8.0 %collective-permute-start.7 = (bf16[80,768]{1,0:T(8,128)(2,1)S(1)}, bf16[80,768]{1,0:T(8,128)(2,1)S(1)}, u32[]{:S(2)}, u32[]{:S(2)}) collective-permute-start(bf16[80,768]{1,0:T(8,128)(2,1)S(1)} %collective-permute-done.6), channel_id=1, source_target_pairs={{0,32},{32,64},{64,96},{96,128},{128,160},{160,192},{192,224},{224... | collective-permute-start | bytes 368648 | tf_op jit(solution)/shard_map/ppermute | solution.py:129
  270.4 15.5 %collective-permute-start.14 = (bf16[80,768]{1,0:T(8,128)(2,1)S(1)}, bf16[80,768]{1,0:T(8,128)(2,1)S(1)}, u32[]{:S(2)}, u32[]{:S(2)}) collective-permute-start(bf16[80,768]{1,0:T(8,128)(2,1)S(1)} %collective-permute-done.13), channel_id=1, source_target_pairs={{32,0},{64,32},{96,64},{128,96},{160,128},{192,160},{224,192},{256... | collective-permute-start | bytes 368648 | tf_op jit(solution)/shard_map/ppermute | solution.py:131
  289.6 12.1 %collective-permute-start.16 = (bf16[256,768]{1,0:T(8,128)(2,1)S(1)}, bf16[256,768]{1,0:T(8,128)(2,1)S(1)}, u32[]{:S(2)}, u32[]{:S(2)}) collective-permute-start(bf16[256,768]{1,0:T(8,128)(2,1)S(1)} %get-tuple-element.10), channel_id=1, source_target_pairs={{0,16},{1,17},{2,18},{3,19},{4,20},{5,21},{6,22},{7,23},{8,24},{9,... | collective-permute-start | bytes 1179656 | tf_op jit(solution)/shard_map/ppermute | solution.py:16
  306.5 57.2 %all-to-all-start.4 = ((bf16[32,40,256]{2,1,0:T(8,128)(2,1)}), bf16[32,40,256]{2,1,0:T(8,128)(2,1)}, u32[]{:S(2)}, u32[]{:S(2)}) async-start(bf16[32,40,256]{2,1,0:T(8,128)(2,1)} %bitcast.119), calls=%async_computation.4 | async-start | bytes 1310720 | tf_op jit(solution)/shard_map/all_to_all | solution.py:143
  325.5 29.1 %copy-start.3 = (bf16[32,40,256]{2,1,0:T(8,128)(2,1)S(1)}, bf16[32,40,256]{2,1,0:T(8,128)(2,1)}, u32[]{:S(2)}) copy-start(bf16[32,40,256]{2,1,0:T(8,128)(2,1)} %copy-done.2) | copy-start | bytes 1966084
  328.5 33.6 %copy-start.8 = (bf16[1,768,256]{2,1,0:T(8,128)(2,1)S(1)}, bf16[1,768,256]{2,1,0:T(8,128)(2,1)}, u32[]{:S(2)}) copy-start(bf16[1,768,256]{2,1,0:T(8,128)(2,1)} %param.14) | copy-start | bytes 1179652
  328.5 50.3 %collective-permute-start.15 = (bf16[256,768]{1,0:T(8,128)(2,1)}, bf16[256,768]{1,0:T(8,128)(2,1)}, u32[]{:S(2)}, u32[]{:S(2)}) collective-permute-start(bf16[256,768]{1,0:T(8,128)(2,1)} %get-tuple-element.8), channel_id=1, source_target_pairs={{0,16},{1,17},{2,18},{3,19},{4,20},{5,21},{6,22},{7,23},{8,24},{9,... | collective-permute-start | bytes 1179656 | tf_op jit(solution)/shard_map/ppermute | solution.py:16
  354.6 7.5 %copy-start.11 = (bf16[1280,768]{1,0:T(8,128)(2,1)S(1)}, bf16[1280,768]{1,0:T(8,128)(2,1)}, u32[]{:S(2)}) copy-start(bf16[1280,768]{1,0:T(8,128)(2,1)} %all-gather.3.cloned.1.call-done) | copy-start | bytes 5898244
  357.8 23.1 %collective-permute-start.17 = (bf16[768,256]{1,0:T(8,128)(2,1)}, bf16[768,256]{1,0:T(8,128)(2,1)}, u32[]{:S(2)}, u32[]{:S(2)}) collective-permute-start(bf16[768,256]{1,0:T(8,128)(2,1)} %get-tuple-element.12), channel_id=1, source_target_pairs={{0,16},{1,17},{2,18},{3,19},{4,20},{5,21},{6,22},{7,23},{8,24},{9,... | collective-permute-start | bytes 1179656 | tf_op jit(solution)/shard_map/ppermute | solution.py:16
  363.7 28.1 %all-to-all-start.1 = ((bf16[32,40,256]{2,1,0:T(8,128)(2,1)}), bf16[32,40,256]{2,1,0:T(8,128)(2,1)S(1)}, u32[]{:S(2)}, u32[]{:S(2)}) async-start(bf16[32,40,256]{2,1,0:T(8,128)(2,1)} %bitcast.7), calls=%async_computation.1 | async-start | bytes 1310720 | tf_op jit(solution)/shard_map/all_to_all | solution.py:104
  378.8 4.0 %copy-start.6 = (pred[1280,128]{1,0:T(8,128)(4,1)S(1)}, pred[1280,128]{1,0:T(8,128)(4,1)}, u32[]{:S(2)}) copy-start(pred[1280,128]{1,0:T(8,128)(4,1)} %copy-done.5) | copy-start | bytes 491524
  378.8 12.9 %copy-start.1 = (f32[1280,128]{1,0:T(8,128)S(1)}, f32[1280,128]{1,0:T(8,128)}, u32[]{:S(2)}) copy-start(f32[1280,128]{1,0:T(8,128)} %select_reduce_fusion) | copy-start | bytes 1966084
Sparse Core Ops, SparseCore 0:
  63.0 148.9 reduce-scatter.3
  214.8 69.2 all-gather.4
  286.4 68.0 all-gather.2
